TPU v7x, 256 devices: a whole 4x4x8 slice. The times are simulated.
256 devices in a mesh: dp: 8 (over z), vocab: 32 (over y, x, core).
Axes of the slice: x: 4, y: 4, z: 8, core: 2. Of those that a mesh axis runs over, the one named last changes fastest.
Arguments:
- hidden: bfloat16 [5120, 4096], P(('dp', 'vocab')), may hold values from -192 to 192, as said below
- out_weight: bfloat16 [4096, 81920], P('dp', 'vocab'), may hold values from -0.09375 to 0.09375
- labels: int32 [5120], P('dp'), may hold values from 0 to 81919
- text_mask: int32 [5120], P('dp'), may hold values from 0 to 1, as said below
Outputs:
- token_loss: float32 [5120], P('dp')
- mean_loss: float32 [], replicated
Inputs may be any that keep to these rules, and one draw needn't show every extreme that they name: The hidden states are of moderate size in most rows, possibly larger in a few. `text_mask`: vision and text tokens come in runs of 16 aligned tokens.
All inputs are finite; a program needn't handle non-finite values.
Results may differ from a plain program's by a relative error of at most 0.0003.
Values may be sent and summed in bfloat16 or wider, within the bound.
A program may use at most 128 MiB of HBM per device.

v0:
```python
import jax
import jax.numpy as jnp
from jax import lax
from jax.sharding import PartitionSpec as P


def from_everyone(x, axis):
    devices = lax.axis_size(axis)
    return lax.all_to_all(jnp.broadcast_to(x[None], (devices, *x.shape)), axis, 0, 0, tiled=True)


def collected_together(x, axis):
    leaves = jax.tree.leaves(x)
    order = sorted(range(len(leaves)), key=lambda k: -leaves[k].size)
    width = (1, *leaves[order[0]].shape)[-1]
    lines = [
        jnp.pad(leaves[k].reshape(-1), (0, -leaves[k].size % width)).reshape(-1, width)
        for k in order
    ]
    both, at, found = (from_everyone(jnp.concatenate(lines), axis), 0, {})
    for k, line in zip(order, lines):
        slab = both[:, at : at + len(line)].reshape(len(both), -1)
        found[k] = slab[:, : leaves[k].size].reshape(-1, *leaves[k].shape)
        at += len(line)
    numbers = iter(range(len(leaves)))
    return jax.tree.map(lambda _: found[next(numbers)], x)


def joined_by_halves(pieces, combine):
    while len(jax.tree.leaves(pieces)[0]) > 1:
        pieces = jax.vmap(combine)(
            *(jax.tree.map(lambda part: part[side::2], pieces) for side in (0, 1))
        )
    return jax.tree.map(lambda part: part[0], pieces)


def joined_all(x, axis, combine):
    pieces = collected_together(x, axis)
    return joined_by_halves(pieces, combine)


def over_copies(x, axis):
    return from_everyone(x, axis).sum(axis=0)


def packed_total(arrays, axis):
    line, at, done = (jnp.concatenate([a.reshape(-1) for a in arrays]), 0, [])
    so_far = over_copies(line, axis)
    for a in arrays:
        done.append(so_far[at : at + a.size].reshape(a.shape))
        at += a.size
    return tuple(done)


def shards(hidden, out_weight, labels, text_mask):
    gathered = lax.all_gather(hidden, "vocab", axis=0, tiled=True)
    width_here = out_weight.shape[1]
    first_column = lax.axis_index("vocab") * width_here
    weight_full = lax.all_gather(out_weight, "dp", axis=0, tiled=True)
    logits = jnp.dot(gathered, weight_full, preferred_element_type=jnp.float32)
    columns = jnp.arange(width_here, dtype=jnp.int32)
    local_targets = labels - first_column
    picked = jnp.sum(
        jnp.where(columns[None, :] == local_targets[:, None], logits, jnp.float32(0.0)), axis=1
    )
    local_top = jnp.max(logits, axis=1)
    weights_text = text_mask.astype(jnp.float32)
    local_total = jnp.sum(jnp.exp(logits - local_top[:, None]), axis=1)

    def combine(first, second):
        upper = jnp.maximum(first[0], second[0])
        summed = first[1] * jnp.exp(first[0] - upper) + second[1] * jnp.exp(second[0] - upper)
        return (upper, summed, first[2] + second[2])

    row_top, exp_total, label_logit = joined_all((local_top, local_total, picked), "vocab", combine)
    token_loss = weights_text * (row_top + jnp.log(exp_total) - label_logit)
    loss_sum, tally = packed_total((jnp.sum(token_loss), jnp.sum(weights_text)), "dp")
    mean_loss = loss_sum / jnp.maximum(tally, jnp.float32(1.0))
    return (token_loss, mean_loss)


def solution(mesh):
    in_specs = (P(("dp", "vocab"), None), P("dp", "vocab"), P("dp"), P("dp"))
    out_specs = (P("dp"), P())
    return jax.shard_map(shards, mesh=mesh, in_specs=in_specs, out_specs=out_specs, check_vma=False)
```

profile of v0, /device:TPU:1, one launch (start us, length us, event | category | flops | bytes accessed | tf_op | source)
XLA Modules:
  0.0 342.3 jit_solution(15762076118572349161)
XLA Ops:
  7.2 0.0 all-gather.6.cloned.1.call-start
  7.2 0.7 all-gather.6.cloned.1.call-update
  7.9 0.0 all-gather.4.cloned.1.call-start
  7.9 0.7 all-gather.4.cloned.1.call-update
  8.7 0.7 broadcast_subtract_fusion
  9.3 59.4 %all-gather.6.cloned.1.call-done = bf16[32,20,4096]{2,1,0:T(8,128)(2,1)} async-done(((bf16[1,20,4096]{2,1,0:T(8,128)(2,1)}), bf16[32,20,4096]{2,1,0:T(8,128)(2,1)}) %all-gather.6.cloned.1.call-update) | async-done | bytes 5242896 | tf_op jit(solution)/shard_map/all_gather | solution.py:56
  68.7 7.8 %reshape.54 = bf16[640,4096]{1,0:T(8,128)(2,1)} reshape(bf16[32,20,4096]{2,1,0:T(8,128)(2,1)} %all-gather.6.cloned.1.call-done) | data formatting | bytes 10485760
  76.5 204.4 %all-gather.4.cloned.1.call-done = bf16[4096,2560]{1,0:T(8,128)(2,1)} async-done(((bf16[512,2560]{1,0:T(8,128)(2,1)}), bf16[4096,2560]{1,0:T(8,128)(2,1)}) %all-gather.4.cloned.1.call-update) | async-done | bytes 20971536 | tf_op jit(solution)/shard_map/all_gather | solution.py:59
  280.9 18.6 %fusion.7 = (f32[640]{0:T(1024)S(1)}, f32[640,2560]{1,0:T(8,128)S(1)}) fusion(bf16[640,4096]{1,0:T(8,128)(2,1)} %reshape.54, bf16[4096,2560]{1,0:T(8,128)(2,1)} %all-gather.4.cloned.1.call-done), kind=kOutput, calls=%fused_computation.26 | convolution fusion | flops 13423410176 | bytes 32770560 | tf_op jit(solution)/shard_map/dot_general | solution.py:60
  299.5 0.0 copy-start
  299.5 1.7 exponential_reduce_fusion
  301.3 17.0 %all_to_all.11 = f32[32,3,640]{2,1,0:T(4,128)S(1)} all-to-all(f32[32,3,640]{2,1,0:T(4,128)S(1)} %broadcast_in_dim.9), channel_id=1, replica_groups=mesh['dp'=8,'vocab'=32] {'vocab'}, dimensions={0} | all-to-all | bytes 491520 | tf_op jit(solution)/shard_map/all_to_all | solution.py:9
  318.3 0.2 fusion.5
  319.3 0.0 copy-done
  319.3 1.3 fusion.4
  320.6 1.4 pad_maximum_fusion.1
  322.0 10.4 %all_to_all.12 = f32[8,1,2]{2,1,0:T(1,128)S(1)} all-to-all(f32[8,1,2]{2,1,0:T(1,128)S(1)} %broadcast_in_dim.10), channel_id=1, replica_groups=mesh['dp'=8,'vocab'=32] {'dp'}, dimensions={0} | all-to-all | bytes 128 | tf_op jit(solution)/shard_map/all_to_all | solution.py:9
  332.4 0.6 fusion.6
  (42 shorter events, 0.8 us)
Async XLA Ops:
  7.2 61.5 %all-gather.6.cloned.1.call-start = ((), (), s32[]{:S(2)}) async-start(), calls=%async_computation.3 | async-start | bytes 6488064 | tf_op jit(solution)/shard_map/all_gather | solution.py:56
  7.9 273.0 %all-gather.4.cloned.1.call-start = ((), (), s32[]{:S(2)}) async-start(), calls=%async_computation.2 | async-start | bytes 23592960 | tf_op jit(solution)/shard_map/all_gather | solution.py:59
  299.5 19.8 %copy-start = (s32[640]{0:T(1024)S(1)}, s32[640]{0:T(1024)}, u32[]{:S(2)}) copy-start(s32[640]{0:T(1024)} %param.7) | copy-start | bytes 7684
Sparse Core Ops, SparseCore 0:
  10.5 58.1 all-gather.5
  70.5 210.3 all-gather.3
where the time goes:
time: 343 us; the launch traced here: 342 us
  waiting for transfers between devices  265 us (77%)
  blocking collectives  27.4 us (8%)
  matrix products  18.6 us (5%)
  between operations  16.7 us (5%)
  local copies, waits for them, and re-layouts  9.13 us (3%)
  other arithmetic  5.29 us (2%)
    all_gather x1, waiting for transfers between devices, shards(): weight_full = lax.all_gather(out_weight, 'dp', axis=0, tiled=True)  204 us
    all_gather x1, waiting for transfers between devices, shards(): gathered = lax.all_gather(hidden, 'vocab', axis=0, tiled=True)  59.4 us
    all_to_all x2, blocking collectives, from_everyone(): lax.all_to_all(jnp.broadcast_to(x[None], (devices, *x.shape)), axis, 0, 0...  27.4 us
    dot_general x1, matrix products, shards(): logits = jnp.dot(gathered, weight_full, preferred_element_type=jnp.float32)  18.6 us
    unnamed x4, local copies, waits for them, and re-layouts  7.78 us
  transfers between devices with their start and end apart: 2, of which 2 were waited for; matrix products, arithmetic and copies ran while one was open for 2% of the time, Pallas kernels for 0%

commit v1 on v0

v1 whole, which is shorter than its diff:
```python
import jax
import jax.numpy as jnp
from jax import lax
from jax.experimental import pallas as pl
from jax.experimental.pallas import tpu as pltpu
from jax.sharding import PartitionSpec as P

NZ, NY, NX, NC = 8, 4, 4, 2
ROWS = 20
D = 4096
KROWS = D // NZ
BLOCK = 640
CH = 128
NQ = BLOCK // CH
GROUP = 8 * ROWS
TOK = NZ * GROUP
SLOTS = 64
LEAST = float(jnp.finfo(jnp.float32).min)
MT = 320


def main_kernel(
    h_ref, w_ref, lab_ref, out_ref,
    raw, act, wbuf, labs, labcol, stage, m_ref, s_ref, p_ref,
    hrecv, hsend, wrecv, wsend, lrecv, lsend, local_sem,
):
    z = lax.axis_index("dp")
    v = lax.axis_index("vocab")
    c = v % 2
    x = (v // 2) % 4
    y = v // 8
    yb = y % 2
    xp, xm = (x + 1) % 4, (x + 3) % 4
    zp, zm = (z + 1) % 8, (z + 7) % 8
    ypair = y + 1 - 2 * yb
    ystar = (y + 2 * yb + 3) % 4

    def dev(zz, yy, xx, cc):
        return {"dp": zz, "vocab": (yy * 4 + xx) * 2 + cc}

    bar = pltpu.get_barrier_semaphore()

    def greet(d):
        pl.semaphore_signal(bar, inc=1, device_id=d, device_id_type=pl.DeviceIdType.MESH)

    @pl.loop(1, 8)
    def _(k):
        greet(dev((z + k) % 8, y, x, c))

    @pl.loop(0, 8)
    def _(k):
        greet(dev((z + k) % 8, y, x, 1 - c))

    greet(dev(z, y, xp, c))
    greet(dev(z, y, xm, c))
    greet(dev(z, ypair, x, c))
    greet(dev(z, ystar, x, c))
    pl.semaphore_wait(bar, 19)

    def slot_of(zs, xs, b):
        return (zs * 4 + xs) * 2 + b

    def h_copy(slot, d):
        return pltpu.make_async_remote_copy(
            src_ref=raw.at[slot], dst_ref=raw.at[slot], send_sem=hsend, recv_sem=hrecv.at[slot],
            device_id=d, device_id_type=pl.DeviceIdType.MESH)

    def h_wait(slot):
        pltpu.make_async_copy(raw.at[slot], raw.at[slot], hrecv.at[slot]).wait()

    to_zp, to_zm = dev(zp, y, x, c), dev(zm, y, x, c)
    to_xp, to_xm = dev(z, y, xp, c), dev(z, y, xm, c)
    to_yp, to_ys = dev(z, ypair, x, c), dev(z, ystar, x, c)
    to_core = dev(z, y, x, 1 - c)

    def z_of(d):
        k = (d + 1) // 2
        return (z + jnp.where(d % 2 == 1, 8 - k, k)) % 8

    def w_at(q, zs, side):
        return wbuf.at[q, pl.ds(pl.multiple_of(zs * KROWS, KROWS), KROWS), pl.ds(side * CH, CH)]

    def w_wait(q, zs, side):
        pltpu.make_async_copy(w_at(q, zs, side), w_at(q, zs, side), wrecv.at[q, zs, side]).wait()

    def w_send(q, zs, side, to_side, d):
        pltpu.make_async_remote_copy(
            src_ref=w_at(q, zs, side), dst_ref=w_at(q, zs, to_side), send_sem=wsend,
            recv_sem=wrecv.at[q, zs, to_side], device_id=d, device_id_type=pl.DeviceIdType.MESH).start()

    tcore = z % 2
    selfish = jnp.logical_and(z // 4 == c, tcore == c)

    def w_first(q):
        @pl.loop(0, 4)
        def _(j):
            p = 4 * c + j
            src = w_ref.at[:, pl.ds(pl.multiple_of(j * BLOCK + q * CH, CH), CH)]
            mine = jnp.logical_and(p == z, tcore == c)

            @pl.when(mine)
            def _():
                pltpu.make_async_copy(src, w_at(q, z, 0), wrecv.at[q, z, 0]).start()

            @pl.when(jnp.logical_not(mine))
            def _():
                pltpu.make_async_remote_copy(
                    src_ref=src, dst_ref=w_at(q, z, 0), send_sem=wsend, recv_sem=wrecv.at[q, z, 0],
                    device_id=dev(p, y, x, tcore), device_id_type=pl.DeviceIdType.MESH).start()

    own_slot = slot_of(z, x, yb)
    own = pltpu.make_async_copy(h_ref, raw.at[own_slot], local_sem)
    own.start()

    own.wait()

    same = (c + z) % 2

    def w_z(n):
        a, b = ((0, 1), (2, 7), (6, 3), (4, 5))[n]
        return (z + jnp.where(same == 0, a, b)) % 8

    def step_a(d):
        zs = z_of(d)
        slot = slot_of(zs, x, yb)

        @pl.when(d > 0)
        def _():
            h_wait(slot)

        even = zs % 2 == 0
        odd_d = d % 2 == 1
        up = (d == 0) | (odd_d & (d <= 3)) | ((d == 5) & even)
        down = (d == 0) | (jnp.logical_not(odd_d) & (d <= 4)) | ((d == 6) & jnp.logical_not(even))

        @pl.when(up)
        def _():
            h_copy(slot, to_zp).start()

        @pl.when(down)
        def _():
            h_copy(slot, to_zm).start()

        h_copy(slot, to_xp).start()
        h_copy(slot, to_xm).start()
        h_copy(slot, to_yp).start()

    def step_b(d):
        zs = z_of(d)
        even = zs % 2 == 0
        s1, s2, s3 = slot_of(zs, xm, yb), slot_of(zs, xp, yb), slot_of(zs, x, 1 - yb)
        h_wait(s1)

        @pl.when(even)
        def _():
            h_copy(s1, to_xp).start()

        @pl.when(c == 0)
        def _():
            h_copy(s1, to_yp).start()

        h_wait(s2)

        @pl.when(jnp.logical_not(even))
        def _():
            h_copy(s2, to_xm).start()

        @pl.when(c == 0)
        def _():
            h_copy(s2, to_yp).start()

        h_wait(s3)

        @pl.when(c == 1)
        def _():
            h_copy(s3, to_xp).start()
            h_copy(s3, to_xm).start()

    def step_c(d):
        zs = z_of(d)
        even = zs % 2 == 0
        s4 = slot_of(zs, (x + 2) % 4, yb)
        s5, s6 = slot_of(zs, xm, 1 - yb), slot_of(zs, xp, 1 - yb)
        h_wait(s4)

        @pl.when(c == 0)
        def _():
            h_copy(s4, to_yp).start()

        h_wait(s5)

        @pl.when((c == 1) & even)
        def _():
            h_copy(s5, to_xp).start()

        h_wait(s6)

        @pl.when((c == 1) & jnp.logical_not(even))
        def _():
            h_copy(s6, to_xm).start()

    def step_d(d):
        zs = z_of(d)
        h_wait(slot_of(zs, (x + 2) % 4, 1 - yb))

        @pl.loop(0, 2)
        def _(g):
            for k in range(4):
                stage[pl.ds(k * ROWS, ROWS), :] = raw[zs * 8 + g * 4 + k].astype(jnp.float32)
            row = pl.multiple_of(zs * GROUP + g * 4 * ROWS, 16)
            act[pl.ds(row, 4 * ROWS), :] = stage[...].astype(jnp.bfloat16)

    def w_direct(i):
        q, half = i // 2, i % 2
        for n in range(2):
            zs = jnp.where(half == 0, w_z(n), w_z(n + 2))
            w_wait(q, zs, 0)
            w_send(q, zs, 0, 1, to_ys)
            w_send(q, zs, 0, 0, to_core)

    def w_across(i):
        q, half = i // 2, i % 2
        for n in range(2):
            zs = jnp.where(half == 0, w_z(n), w_z(n + 2))
            w_wait(q, zs, 1)
            w_send(q, zs, 1, 1, to_core)

    step_a(jnp.int32(0))
    w_first(0)
    keep = pltpu.make_async_copy(lab_ref, labs.at[z], local_sem)
    keep.start()
    keep.wait()

    def lab_copy(k, zz):
        return pltpu.make_async_remote_copy(
            src_ref=lab_ref, dst_ref=labs.at[zz], send_sem=lsend, recv_sem=lrecv.at[zz],
            device_id=dev((z + k) % 8, y, x, c), device_id_type=pl.DeviceIdType.MESH)

    @pl.loop(1, 8)
    def _(k):
        lab_copy(k, z).start()

    @pl.loop(0, 11)
    def _(i):
        @pl.when((i % 2 == 0) & (i < 2 * NQ - 2))
        def _():
            w_first(i // 2 + 1)

        @pl.when((i >= 1) & (i < 8))
        def _():
            step_a(i)

        @pl.when((i >= 1) & (i < 9))
        def _():
            step_b(i - 1)

        @pl.when(i < 2 * NQ)
        def _():
            w_direct(i)

        @pl.when((i >= 2) & (i < 10))
        def _():
            step_c(i - 2)

        @pl.when(i >= 1)
        def _():
            w_across(i - 1)

        @pl.when(i >= 3)
        def _():
            step_d(i - 3)

    @pl.loop(1, 8)
    def _(k):
        zz = (z + k) % 8
        pltpu.make_async_copy(labs.at[zz], labs.at[zz], lrecv.at[zz]).wait()

    pltpu.make_async_copy(labs.at[pl.ds(0, 7)], labs.at[pl.ds(0, 7)], lsend).wait()

    @pl.loop(0, 8)
    def _(zz):
        line = jnp.broadcast_to(labs[zz][0:1, :], (128, 256))
        labcol[pl.ds(pl.multiple_of(zz * GROUP, 8), GROUP), :] = jnp.transpose(line)[:GROUP]

    m_ref[...] = jnp.full_like(m_ref, LEAST)
    s_ref[...] = jnp.zeros_like(s_ref)
    p_ref[...] = jnp.zeros_like(p_ref)
    lane = lax.broadcasted_iota(jnp.int32, (MT, 128), 1)

    @pl.loop(0, NQ)
    def _(q):
        @pl.loop(0, 4)
        def _(n):
            zs = (1 - c) + 2 * n
            w_wait(q, zs, 0)
            w_wait(q, zs, 1)

        @pl.loop(0, TOK // MT)
        def _(t):
            rows = pl.ds(pl.multiple_of(t * MT, MT), MT)
            logits = jnp.dot(act[rows, :], wbuf[q], preferred_element_type=jnp.float32)
            a, b = logits[:, :CH], logits[:, CH:]
            first = z * BLOCK + q * CH
            target = labcol[rows, :] - lane
            at_a = target == (y * 4 + x) * (8 * BLOCK) + first
            at_b = target == (ystar * 4 + x) * (8 * BLOCK) + first
            p_ref[rows, :] += jnp.where(at_a, a, 0.0) + jnp.where(at_b, b, 0.0)
            old = m_ref[rows, :]
            new = jnp.maximum(old, jnp.maximum(a, b))
            m_ref[rows, :] = new
            s_ref[rows, :] = s_ref[rows, :] * jnp.exp(old - new) + (jnp.exp(a - new) + jnp.exp(b - new))

    @pl.loop(0, 8)
    def _(zz):
        rows = pl.ds(pl.multiple_of(zz * GROUP, 8), GROUP)
        m = m_ref[rows, :]
        top = jnp.max(m, axis=1, keepdims=True)
        total = jnp.sum(s_ref[rows, :] * jnp.exp(m - top), axis=1, keepdims=True)
        got = jnp.sum(p_ref[rows, :], axis=1, keepdims=True)
        ids = lax.broadcasted_iota(jnp.int32, (GROUP, 128), 1)
        packed = jnp.where(ids == 0, top, jnp.where(ids == 1, total, got))
        packed = jnp.concatenate([packed, jnp.zeros((256 - GROUP, 128), jnp.float32)], axis=0)
        out_ref[zz] = jnp.transpose(packed)[:8]

    pltpu.make_async_copy(raw.at[pl.ds(0, 63)], raw.at[pl.ds(0, 63)], hsend).wait()

    @pl.when(selfish)
    def _():
        part = wbuf.at[:, pl.ds(0, D - 256), :]
        pltpu.make_async_copy(part, part, wsend).wait()

    @pl.when(jnp.logical_not(selfish))
    def _():
        pltpu.make_async_copy(wbuf, wbuf, wsend).wait()


def partial_stats(hidden, weight, labels):
    return pl.pallas_call(
        main_kernel,
        out_shape=jax.ShapeDtypeStruct((8, 8, 256), jnp.float32),
        in_specs=[
            pl.BlockSpec(memory_space=pl.ANY),
            pl.BlockSpec(memory_space=pl.ANY),
            pl.BlockSpec(memory_space=pltpu.VMEM),
        ],
        out_specs=pl.BlockSpec(memory_space=pltpu.VMEM),
        scratch_shapes=[
            pltpu.VMEM((SLOTS, ROWS, D), jnp.bfloat16),
            pltpu.VMEM((TOK, D), jnp.bfloat16),
            pltpu.VMEM((NQ, D, 2 * CH), jnp.bfloat16),
            pltpu.VMEM((8, 8, 256), jnp.int32),
            pltpu.VMEM((TOK, 128), jnp.int32),
            pltpu.VMEM((4 * ROWS, D), jnp.float32),
            pltpu.VMEM((TOK, 128), jnp.float32),
            pltpu.VMEM((TOK, 128), jnp.float32),
            pltpu.VMEM((TOK, 128), jnp.float32),
            pltpu.SemaphoreType.DMA((SLOTS,)),
            pltpu.SemaphoreType.DMA,
            pltpu.SemaphoreType.DMA((NQ, 8, 2)),
            pltpu.SemaphoreType.DMA,
            pltpu.SemaphoreType.DMA((8,)),
            pltpu.SemaphoreType.DMA,
            pltpu.SemaphoreType.DMA,
        ],
        compiler_params=pltpu.CompilerParams(
            collective_id=0, has_side_effects=True, vmem_limit_bytes=60 * 2**20),
        name="gather_and_score",
    )(hidden, weight, labels)


def from_everyone(x, axis):
    devices = lax.axis_size(axis)
    return lax.all_to_all(jnp.broadcast_to(x[None], (devices, *x.shape)), axis, 0, 0, tiled=True)


def merged(stats, axes):
    top = jnp.max(stats[..., 0, :], axis=axes, keepdims=True)
    total = jnp.sum(stats[..., 1, :] * jnp.exp(stats[..., 0, :] - top), axis=axes)
    return jnp.stack([jnp.squeeze(top, axes), total, jnp.sum(stats[..., 2, :], axis=axes)], axis=-2)


def shards(hidden, out_weight, labels, text_mask):
    v = lax.axis_index("vocab")
    core, pair = v % 2, v // 16
    mine = labels.reshape(2, 2, 4, 2, ROWS).transpose(0, 3, 2, 1, 4).reshape(4, GROUP)
    mine = lax.dynamic_slice_in_dim(mine, pair * 2 + core, 1, 0)
    mine = jnp.broadcast_to(jnp.pad(mine, ((0, 0), (0, 256 - GROUP))), (8, 256))
    stats = partial_stats(hidden, out_weight, mine)
    stats = lax.all_to_all(stats, "dp", 0, 0, tiled=True)[:, :3, :GROUP]
    stats = from_everyone(merged(stats, 0), "vocab")
    stats = merged(stats.reshape(2, 2, 4, 2, 3, GROUP), (1, 2))
    loss = stats[:, :, 0] + jnp.log(stats[:, :, 1]) - stats[:, :, 2]
    loss = loss.reshape(2, 2, 4, 2, ROWS).transpose(0, 3, 2, 1, 4).reshape(-1)
    weights_text = text_mask.astype(jnp.float32)
    token_loss = weights_text * loss
    sums = jnp.stack([jnp.sum(token_loss), jnp.sum(weights_text)])
    loss_sum, tally = from_everyone(sums, "dp").sum(axis=0)
    mean_loss = loss_sum / jnp.maximum(tally, jnp.float32(1.0))
    return (token_loss, mean_loss)


def solution(mesh):
    in_specs = (P(("dp", "vocab"), None), P("dp", "vocab"), P("dp"), P("dp"))
    out_specs = (P("dp"), P())
    return jax.shard_map(shards, mesh=mesh, in_specs=in_specs, out_specs=out_specs, check_vma=False)
```

time: 343 us -> 182 us (0.53)
  waiting for transfers between devices: 265 us -> 0 us
  Pallas kernels: 0 us -> 133 us
  matrix products: 18.6 us -> 0 us
  between operations: 16.7 us -> 3.25 us
  blocking collectives: 27.4 us -> 39 us
  local copies, waits for them, and re-layouts: 9.13 us -> 3.18 us
    all_gather x2 -> x0, waiting for transfers between devices: 264 us -> none  [the longest x1 204 us: shards(): weight_full = lax.all_gather(out_weight, 'dp', axis=0, tiled=True)]
    pallas_call x0 -> x1, Pallas kernels: none -> 133 us  [partial_stats(): pl.pallas_call(main_kernel, out_shape=jax.ShapeDtypeStruct((8, 8, 256), j...]
    dot_general x1 -> x0, matrix products: 18.6 us -> none  [shards(): logits = jnp.dot(gathered, weight_full, preferred_element_type=jnp.float32)]
    all_to_all x0 -> x1, blocking collectives: none -> 11.3 us  [shards(): stats = lax.all_to_all(stats, 'dp', 0, 0, tiled=True)[:, :3, :GROUP]]
    unnamed x4, local copies, waits for them, and re-layouts: 7.78 us -> 0.34 us
  transfers between devices with their start and end apart: 2 -> 0, of which waited for: 2 -> 0; matrix products, arithmetic and copies ran while one was open for 2% -> 0% of each run, Pallas kernels for 0% -> 0%
where the time goes in v1:
time: 182 us
  Pallas kernels  133 us (73%)
  blocking collectives  39 us (21%)
  other arithmetic  3.76 us (2%)
  between operations  3.25 us (2%)
  local copies, waits for them, and re-layouts  3.18 us (2%)
    pallas_call x1, Pallas kernels, partial_stats(): pl.pallas_call(main_kernel, out_shape=jax.ShapeDtypeStruct((8, 8, 256), j...  133 us
    all_to_all x2, blocking collectives, from_everyone(): lax.all_to_all(jnp.broadcast_to(x[None], (devices, *x.shape)), axis, 0, 0...  27.7 us
    all_to_all x1, blocking collectives, shards(): stats = lax.all_to_all(stats, 'dp', 0, 0, tiled=True)[:, :3, :GROUP]  11.3 us

profile of v1, /device:TPU:1, one launch (start us, length us, event | category | flops | bytes accessed | tf_op | source)
XLA Modules:
  0.0 181.8 jit_solution(1563284221768899764)
XLA Ops:
  0.6 0.0 copy-start
  0.7 0.8 reshape.35
  1.5 0.1 reshape.36
  1.6 0.6 broadcast_in_dim.11.lab_ref
  2.2 132.5 %gather_and_score.1 = f32[8,8,256]{2,1,0:T(8,128)} custom-call(bf16[20,4096]{1,0:T(8,128)(2,1)} %h_ref.1, bf16[512,2560]{1,0:T(8,128)(2,1)} %w_ref.1, s32[8,256]{1,0:T(8,128)} %broadcast_in_dim.11.lab_ref), custom_call_target="tpu_custom_call" | custom-call | tf_op jit(solution)/shard_map/gather_and_score/pallas_call | solution.py:338
  134.7 11.3 %all_to_all.16 = f32[8,8,256]{2,1,0:T(8,128)S(1)} all-to-all(f32[8,8,256]{2,1,0:T(8,128)} %gather_and_score.1), channel_id=1, replica_groups=mesh['dp'=8,'vocab'=32] {'dp'}, dimensions={0} | all-to-all | bytes 131072 | tf_op jit(solution)/shard_map/all_to_all | solution.py:389
  146.1 0.2 reshape.39
  146.4 18.8 %all_to_all.17 = f32[32,1,480]{2,1,0:T(1,128)S(1)} all-to-all(f32[32,1,480]{2,1,0:T(1,128)S(1)} %reshape.39), channel_id=1, replica_groups=mesh['dp'=8,'vocab'=32] {'vocab'}, dimensions={0} | all-to-all | bytes 122880 | tf_op jit(solution)/shard_map/all_to_all | solution.py:373
  165.2 0.5 broadcast.10
  165.7 0.8 reduce.5
  166.5 0.1 reshape.40
  166.6 0.1 fusion.9
  166.8 0.1 sub.33
  166.9 0.1 reshape.38
  167.0 0.0 copy-done
  167.1 1.3 fusion.8
  168.3 1.4 pad_maximum_fusion.1
  169.8 8.9 %all_to_all.18 = f32[8,1,2]{2,1,0:T(1,128)S(1)} all-to-all(f32[8,1,2]{2,1,0:T(1,128)S(1)} %broadcast_in_dim.27), channel_id=1, replica_groups=mesh['dp'=8,'vocab'=32] {'dp'}, dimensions={0} | all-to-all | bytes 128 | tf_op jit(solution)/shard_map/all_to_all | solution.py:373
  178.7 0.6 fusion.10
  (12 shorter events, 0.2 us)
Async XLA Ops:
  0.6 166.4 %copy-start = (s32[640]{0:T(1024)S(1)}, s32[640]{0:T(1024)}, u32[]{:S(2)}) copy-start(s32[640]{0:T(1024)} %param.7) | copy-start | bytes 7684

commit v2 on v1

v2 whole, which is shorter than its diff:
```python
import functools

import jax
import jax.numpy as jnp
from jax import lax
from jax.experimental import pallas as pl
from jax.experimental.pallas import tpu as pltpu
from jax.sharding import PartitionSpec as P

ROWS = 20
D = 4096
KROWS = D // 8
BLOCK = 640
CH = 128
NQ = BLOCK // CH
GROUP = 8 * ROWS
TOK = 8 * GROUP
LEAST = float(jnp.finfo(jnp.float32).min)
MT = 320
RING = (8, 8, 18, 18, 27, 27, 42)
SPREAD = (8, 13, 20, 27, 34, 42, 50)
ROUND1 = (6, 14, 20, 28, 35, 43, 51, 58)
ROUND2 = (18, 25, 32, 38, 46, 53, 60, 66)
ROUND3 = (26, 34, 42, 49, 57, 63, 69, 75)
SEND = (0, 8, 18, 27, 32, 37, 43, 48, 53, 58)
DIRECT = (12, 20, 29, 37, 43, 48, 54, 60, 65, 71)
ACROSS = (21, 29, 38, 46, 52, 57, 63, 69, 74, 80)
OTHER = (31, 48, 59, 71, 82)
CELLS = ((0, 0, 40), (1, 0, 52), (0, 1, 52), (1, 1, 56), (0, 2, 60), (1, 2, 64), (2, 0, 64), (2, 1, 68), (2, 2, 68), (0, 3, 72), (1, 3, 72), (2, 3, 76), (3, 0, 76), (3, 1, 76), (3, 2, 77), (3, 3, 77))
STEP_US = 4
STEPS = 82 // STEP_US + 1
MESH = pl.DeviceIdType.MESH


def pick(n, values):
    out = jnp.int32(values[0])
    for k in range(1, len(values)):
        if values[k] != values[k - 1]:
            out = jnp.where(n >= k, jnp.int32(values[k]), out)
    return out


def joined(tiles):
    top = functools.reduce(jnp.maximum, [t[0:2] for t in tiles])
    total = functools.reduce(jnp.add, [t[2:4] * jnp.exp(t[0:2] - top) for t in tiles])
    got = functools.reduce(jnp.add, [t[4:6] for t in tiles])
    return top, total, got


def main_kernel(
    h_ref, w_ref, lab_ref, mask_ref, loss_ref, mean_ref,
    act, braw, wbuf, mine, perm, lab_out, mask_in, loss_in, labs, labcol, stage, m_ref, s_ref, p_ref,
    out1, in1, out2, in2, out3, in3,
    hrecv, hsend, wrecv, wsend, lrecv, lsend, local_sem, fsend, frecv,
):
    z = lax.axis_index("dp")
    v = lax.axis_index("vocab")
    c = v % 2
    x = (v // 2) % 4
    y = v // 8
    yb = y % 2
    xp, xm = (x + 1) % 4, (x + 3) % 4
    zp, zm = (z + 1) % 8, (z + 7) % 8
    ypair = y + 1 - 2 * yb
    ystar = (y + 2 * yb + 3) % 4

    def dev(zz, yy, xx, cc):
        return {"dp": zz, "vocab": (yy * 4 + xx) * 2 + cc}

    bar = pltpu.get_barrier_semaphore()

    def greet(d):
        pl.semaphore_signal(bar, inc=1, device_id=d, device_id_type=MESH)

    @pl.loop(1, 8)
    def _(k):
        greet(dev((z + k) % 8, y, x, c))
        greet(dev((z + k) % 8, y, x, 1 - c))

    @pl.loop(1, 32)
    def _(k):
        greet({"dp": z, "vocab": (v + k) % 32})

    def rows_of(d, piece):
        return pl.ds(pl.multiple_of(d * GROUP + piece * 16, 16), 16)

    own = x * 2 + yb
    first = pltpu.make_async_copy(h_ref.at[pl.ds(0, 16)], act.at[rows_of(0, own)], local_sem)
    first.start()
    second = pltpu.make_async_copy(h_ref, mine, lsend)
    second.start()
    second.wait()
    few = mine[...].astype(jnp.float32)[16:ROWS]
    for kq in range(4):
        stage[kq * 4 : kq * 4 + 4, 0 : D // 4] = few[:, kq * (D // 4) : (kq + 1) * (D // 4)]
    braw[own] = stage[:, 0 : D // 4].astype(jnp.bfloat16)
    first.wait()
    pl.semaphore_wait(bar, 45)

    def h_copy(d, piece, to_d, device):
        for src, dst in (
            (act.at[rows_of(d, piece)], act.at[rows_of(to_d, piece)]),
            (braw.at[d * 8 + piece], braw.at[to_d * 8 + piece]),
        ):
            pltpu.make_async_remote_copy(
                src_ref=src, dst_ref=dst, send_sem=hsend, recv_sem=hrecv.at[to_d * 8 + piece],
                device_id=device, device_id_type=MESH).start()

    def h_wait(d, piece):
        size = wbuf.at[0, pl.ds(0, 320), :]
        pltpu.make_async_copy(size, size, hrecv.at[d * 8 + piece]).wait()

    to_zp, to_zm = dev(zp, y, x, c), dev(zm, y, x, c)
    to_xp, to_xm = dev(z, y, xp, c), dev(z, y, xm, c)
    to_yp, to_ys = dev(z, ypair, x, c), dev(z, ystar, x, c)
    to_core = dev(z, y, x, 1 - c)

    def z_of(d):
        k = (d + 1) // 2
        return (z + jnp.where(d % 2 == 1, 8 - k, k)) % 8

    def w_at(q, zs, side):
        return wbuf.at[q, pl.ds(pl.multiple_of(zs * KROWS, KROWS), KROWS), pl.ds(side * CH, CH)]

    def w_wait(q, zs, side):
        pltpu.make_async_copy(w_at(q, zs, side), w_at(q, zs, side), wrecv.at[q, zs, side]).wait()

    def w_send(q, zs, side, to_side, d):
        pltpu.make_async_remote_copy(
            src_ref=w_at(q, zs, side), dst_ref=w_at(q, zs, to_side), send_sem=wsend,
            recv_sem=wrecv.at[q, zs, to_side], device_id=d, device_id_type=MESH).start()

    tcore = z % 2
    selfish = jnp.logical_and(z // 4 == c, tcore == c)

    def w_first(i):
        q, half = i // 2, i % 2

        def one(j):
            p = 4 * c + j
            src = w_ref.at[:, pl.ds(pl.multiple_of(j * BLOCK + q * CH, CH), CH)]
            mine = jnp.logical_and(p == z, tcore == c)

            @pl.when(mine)
            def _():
                pltpu.make_async_copy(src, w_at(q, z, 0), wrecv.at[q, z, 0]).start()

            @pl.when(jnp.logical_not(mine))
            def _():
                pltpu.make_async_remote_copy(
                    src_ref=src, dst_ref=w_at(q, z, 0), send_sem=wsend, recv_sem=wrecv.at[q, z, 0],
                    device_id=dev(p, y, x, tcore), device_id_type=MESH).start()

        @pl.loop(0, 4)
        def _(j):
            away = (4 * c + j - z + 8) % 8

            @pl.when(((away <= 2) | (away >= 6)) == (half == 0))
            def _():
                one(j)

    same = (c + z) % 2

    def w_z(n):
        a, b = ((0, 1), (2, 7), (6, 3), (4, 5))[n]
        return (z + jnp.where(same == 0, a, b)) % 8

    def x_first(zs):
        return (c == 0) & (zs != 7)

    def ring(d):
        @pl.when(d > 0)
        def _():
            h_wait(d, own)

        even = z_of(d) % 2 == 0
        odd_d = d % 2 == 1
        up = (d == 0) | (odd_d & (d <= 3)) | ((d == 5) & even)
        down = (d == 0) | (jnp.logical_not(odd_d) & (d <= 4)) | ((d == 6) & jnp.logical_not(even))

        @pl.when(up)
        def _():
            h_copy(d, own, jnp.where(d == 0, 1, d + 2), to_zp)

        @pl.when(down)
        def _():
            h_copy(d, own, jnp.where(d == 6, 7, d + 2), to_zm)

    def step_a(d):
        h_copy(d, own, d, to_xp)
        h_copy(d, own, d, to_xm)
        h_copy(d, own, d, to_yp)

    def step_b(d):
        zs = z_of(d)
        even = zs % 2 == 0
        xf = x_first(zs)
        s1, s2, s3 = xm * 2 + yb, xp * 2 + yb, x * 2 + 1 - yb
        h_wait(d, s1)

        @pl.when(even)
        def _():
            h_copy(d, s1, d, to_xp)

        @pl.when(xf)
        def _():
            h_copy(d, s1, d, to_yp)

        h_wait(d, s2)

        @pl.when(jnp.logical_not(even))
        def _():
            h_copy(d, s2, d, to_xm)

        @pl.when(xf)
        def _():
            h_copy(d, s2, d, to_yp)

        h_wait(d, s3)

        @pl.when(jnp.logical_not(xf))
        def _():
            h_copy(d, s3, d, to_xp)
            h_copy(d, s3, d, to_xm)

    def step_c(d):
        zs = z_of(d)
        even = zs % 2 == 0
        xf = x_first(zs)
        s4 = ((x + 2) % 4) * 2 + yb
        s5, s6 = xm * 2 + 1 - yb, xp * 2 + 1 - yb
        h_wait(d, s4)

        @pl.when(xf)
        def _():
            h_copy(d, s4, d, to_yp)

        h_wait(d, s5)

        @pl.when(jnp.logical_not(xf) & even)
        def _():
            h_copy(d, s5, d, to_xp)

        h_wait(d, s6)

        @pl.when(jnp.logical_not(xf) & jnp.logical_not(even))
        def _():
            h_copy(d, s6, d, to_xm)

    def step_d(d):
        h_wait(d, ((x + 2) % 4) * 2 + 1 - yb)

        @pl.loop(0, 2)
        def _(g):
            for k in range(4):
                piece = braw[d * 8 + g * 4 + k].astype(jnp.float32)
                for kq in range(4):
                    stage[pl.ds(k * 4, 4), pl.ds(kq * 1024, 1024)] = piece[kq * 4 : kq * 4 + 4]
            row = pl.multiple_of(d * GROUP + 128 + g * 16, 16)
            act[pl.ds(row, 16), :] = stage[...].astype(jnp.bfloat16)

    def w_direct(i):
        q, half = i // 2, i % 2
        for n in range(2):
            zs = jnp.where(half == 0, w_z(n), w_z(n + 2))
            w_wait(q, zs, 0)
            w_send(q, zs, 0, 1, to_ys)
            w_send(q, zs, 0, 0, to_core)

    def w_across(i):
        q, half = i // 2, i % 2
        for n in range(2):
            zs = jnp.where(half == 0, w_z(n), w_z(n + 2))
            w_wait(q, zs, 1)
            w_send(q, zs, 1, 1, to_core)

    def w_other(q):
        @pl.loop(0, 4)
        def _(n):
            zs = (1 - c) + 2 * n
            w_wait(q, zs, 0)
            w_wait(q, zs, 1)

    lane = lax.broadcasted_iota(jnp.int32, (MT, 128), 1)
    col_a = (y * 4 + x) * (8 * BLOCK) + z * BLOCK
    col_b = (ystar * 4 + x) * (8 * BLOCK) + z * BLOCK

    def cell(t, q):
        rows = pl.ds(pl.multiple_of(t * MT, MT), MT)
        logits = jnp.dot(act[rows, :], wbuf[q], preferred_element_type=jnp.float32)
        a, b = logits[:, :CH], logits[:, CH:]
        target = labcol[rows, :] - lane
        at_a = target == col_a + q * CH
        at_b = target == col_b + q * CH
        p_ref[rows, :] += jnp.where(at_a, a, 0.0) + jnp.where(at_b, b, 0.0)
        old = m_ref[rows, :]
        new = jnp.maximum(old, jnp.maximum(a, b))
        m_ref[rows, :] = new
        s_ref[rows, :] = s_ref[rows, :] * jnp.exp(old - new) + (jnp.exp(a - new) + jnp.exp(b - new))

    ring(jnp.int32(0))
    step_a(jnp.int32(0))

    def place(t):
        piece = (t * 3277) >> 16
        r = t - piece * ROWS
        s8 = ((piece >> 1) & 3) * 2 + ((piece >> 3) & 1)
        group = (piece >> 4) * 2 + (piece & 1)
        head = r < 16
        return jnp.where(head, s8 * 16 + r, s8 * 4 + r - 16), group * 2 + jnp.where(head, 0, 1)

    tile_row = lax.broadcasted_iota(jnp.int32, (8, 128), 0)
    tile_lane = lax.broadcasted_iota(jnp.int32, (8, 128), 1)

    def is_row(k):
        return place(k * 128 + tile_lane)[1] == tile_row

    for k in range(5):
        ids = lax.broadcasted_iota(jnp.int32, (128, 128), 0) + k * 128
        lanes = lax.broadcasted_iota(jnp.int32, (128, 128), 1)
        perm[k] = jnp.where(place(ids)[0] == lanes, 1.0, 0.0)

    def by_piece(ref):
        out = jnp.zeros((8, 128), jnp.float32)
        for k in range(5):
            line = jnp.broadcast_to(ref[k : k + 1].astype(jnp.float32), (8, 128))
            out += jnp.dot(
                jnp.where(is_row(k), line, 0.0), perm[k],
                preferred_element_type=jnp.float32, precision=lax.Precision.HIGHEST)
        return out

    mask_in[...] = by_piece(mask_ref)
    labels = by_piece(lab_ref)
    group = (y // 2) * 2 + c
    lines = [
        jnp.sum(jnp.where(tile_row == group * 2 + k, labels, 0.0), axis=0, keepdims=True) for k in range(2)
    ]
    lab_out[...] = jnp.where(tile_row == 0, lines[0], lines[1]).astype(jnp.int32)

    @pl.loop(1, 8)
    def _(k):
        pltpu.make_async_remote_copy(
            src_ref=lab_out, dst_ref=labs.at[z], send_sem=lsend, recv_sem=lrecv,
            device_id=dev((z + k) % 8, y, x, c), device_id_type=MESH).start()

    labs[z] = lab_out[...]
    m_ref[...] = jnp.full_like(m_ref, LEAST)
    s_ref[...] = jnp.zeros_like(s_ref)
    p_ref[...] = jnp.zeros_like(p_ref)

    def at_step(i, times, body):
        ready = [sum(1 for k in times if k // STEP_US < n) for n in range(STEPS + 1)]
        pl.loop(pick(i, ready[:-1]), pick(i, ready[1:]))(body)

    @pl.loop(0, STEPS)
    def _(i):
        at_step(i, RING, lambda n: ring(n + 1))
        at_step(i, SPREAD, lambda n: step_a(n + 1))
        at_step(i, SEND, w_first)
        at_step(i, ROUND1, step_b)
        at_step(i, DIRECT, w_direct)
        at_step(i, ROUND2, step_c)
        at_step(i, ACROSS, w_across)
        at_step(i, OTHER, w_other)

        @pl.when(i == 5)
        def _():
            seven = labs.at[pl.ds(0, 7)]
            pltpu.make_async_copy(seven, seven, lrecv).wait()
            pltpu.make_async_copy(seven, seven, lsend).wait()

            @pl.loop(0, 8)
            def _(d):
                pair = labs[z_of(d)]
                for k, size in ((0, 128), (1, 32)):
                    line = jnp.transpose(jnp.broadcast_to(pair[k : k + 1], (128, 128)))
                    labcol[pl.ds(pl.multiple_of(d * GROUP + k * 128, 32), size), :] = line[:size]

        at_step(
            i, [k[2] for k in CELLS],
            lambda n: cell(pick(n, [k[0] for k in CELLS]), pick(n, [k[1] for k in CELLS])))
        at_step(i, ROUND3, step_d)

    ids = lax.broadcasted_iota(jnp.int32, (128, 128), 1)

    def to_owner(d):
        columns = []
        for base, size in ((0, 128), (128, 32)):
            rows = pl.ds(pl.multiple_of(d * GROUP + base, 32), size)
            m = m_ref[rows, :]
            top = jnp.max(m, axis=1, keepdims=True)
            total = jnp.sum(s_ref[rows, :] * jnp.exp(m - top), axis=1, keepdims=True)
            got = jnp.sum(p_ref[rows, :], axis=1, keepdims=True)
            columns.append((top, total, got))
        packed = jnp.zeros((128, 128), jnp.float32)
        for k in range(3):
            packed = jnp.where(ids == 2 * k, columns[0][k], packed)
            fill = jnp.full((96, 1), 1.0 if k == 1 else 0.0, jnp.float32)
            packed = jnp.where(ids == 2 * k + 1, jnp.concatenate([columns[1][k], fill], axis=0), packed)
        out1[d] = jnp.transpose(packed)[:8]

        @pl.when(d > 0)
        def _():
            pltpu.make_async_remote_copy(
                src_ref=out1.at[d], dst_ref=in1.at[z], send_sem=fsend.at[0], recv_sem=frecv.at[0],
                device_id=dev(z_of(d), y, x, c), device_id_type=MESH).start()

    @pl.loop(0, 4)
    def _(k):
        t = 3 - k
        cell(t, NQ - 1)
        to_owner(2 * t + 1)
        to_owner(2 * t)

    in1[z] = out1[0]
    seven = in1.at[pl.ds(0, 7)]
    pltpu.make_async_copy(seven, seven, frecv.at[0]).wait()
    top, total, got = joined([in1[k] for k in range(8)])
    out2[0:2, :] = top
    out2[2:4, :] = total
    out2[4:6, :] = got
    out2[6:8, :] = got

    @pl.loop(1, 32)
    def _(k):
        pltpu.make_async_remote_copy(
            src_ref=out2, dst_ref=in2.at[v], send_sem=fsend.at[1], recv_sem=frecv.at[1],
            device_id={"dp": z, "vocab": (v + k) % 32}, device_id_type=MESH).start()

    in2[v] = out2[...]
    many = in2.at[pl.ds(0, 31)]
    pltpu.make_async_copy(many, many, frecv.at[1]).wait()
    for pair in range(2):
        for core in range(2):
            tiles = [in2[((pair * 2 + k // 4) * 4 + k % 4) * 2 + core] for k in range(8)]
            top, total, got = joined(tiles)
            at = (pair * 2 + core) * 2
            loss_in[at : at + 2, :] = mask_in[at : at + 2, :] * (top + jnp.log(total) - got)
    loss_sum = jnp.sum(loss_in[...], axis=(0, 1), keepdims=True)
    tally = jnp.sum(mask_in[...], axis=(0, 1), keepdims=True)
    out3[0:4, :] = jnp.broadcast_to(loss_sum, (4, 128))
    out3[4:8, :] = jnp.broadcast_to(tally, (4, 128))

    @pl.loop(1, 8)
    def _(k):
        pltpu.make_async_remote_copy(
            src_ref=out3, dst_ref=in3.at[z], send_sem=fsend.at[2], recv_sem=frecv.at[2],
            device_id=dev((z + k) % 8, y, x, c), device_id_type=MESH).start()

    in3[z] = out3[...]
    losses = loss_in[...]
    for k in range(5):
        moved = lax.dot_general(
            losses, perm[k], (((1,), (1,)), ((), ())),
            preferred_element_type=jnp.float32, precision=lax.Precision.HIGHEST)
        loss_ref[k : k + 1, :] = jnp.sum(jnp.where(is_row(k), moved, 0.0), axis=0, keepdims=True)
    seven3 = in3.at[pl.ds(0, 7)]
    pltpu.make_async_copy(seven3, seven3, frecv.at[2]).wait()
    sums = functools.reduce(jnp.add, [in3[k] for k in range(8)])
    mean_ref[...] = sums[0:1, 0:1] / jnp.maximum(sums[4:5, 0:1], 1.0)

    pltpu.make_async_copy(seven, seven, fsend.at[0]).wait()
    pltpu.make_async_copy(many, many, fsend.at[1]).wait()
    pltpu.make_async_copy(seven3, seven3, fsend.at[2]).wait()
    hidden_bytes = wbuf.at[:, pl.ds(0, 63 * 64), :]
    pltpu.make_async_copy(hidden_bytes, hidden_bytes, hsend).wait()

    @pl.when(selfish)
    def _():
        part = wbuf.at[:, pl.ds(0, D - 256), :]
        pltpu.make_async_copy(part, part, wsend).wait()

    @pl.when(jnp.logical_not(selfish))
    def _():
        pltpu.make_async_copy(wbuf, wbuf, wsend).wait()


def scored(hidden, weight, labels, mask):
    vmem = pl.BlockSpec(memory_space=pltpu.VMEM)
    anywhere = pl.BlockSpec(memory_space=pl.ANY)
    return pl.pallas_call(
        main_kernel,
        out_shape=(jax.ShapeDtypeStruct((5, 128), jnp.float32), jax.ShapeDtypeStruct((1, 1), jnp.float32)),
        in_specs=[anywhere, anywhere, vmem, vmem],
        out_specs=(vmem, vmem),
        scratch_shapes=[
            pltpu.VMEM((TOK, D), jnp.bfloat16),
            pltpu.VMEM((64, 16, D // 4), jnp.bfloat16),
            pltpu.VMEM((NQ, D, 2 * CH), jnp.bfloat16),
            pltpu.VMEM((ROWS, D), jnp.bfloat16),
            pltpu.VMEM((5, 128, 128), jnp.float32),
            pltpu.VMEM((8, 128), jnp.int32),
            pltpu.VMEM((8, 128), jnp.float32),
            pltpu.VMEM((8, 128), jnp.float32),
            pltpu.VMEM((8, 8, 128), jnp.int32),
            pltpu.VMEM((TOK, 128), jnp.int32),
            pltpu.VMEM((16, D), jnp.float32),
            pltpu.VMEM((TOK, 128), jnp.float32),
            pltpu.VMEM((TOK, 128), jnp.float32),
            pltpu.VMEM((TOK, 128), jnp.float32),
            pltpu.VMEM((8, 8, 128), jnp.float32),
            pltpu.VMEM((8, 8, 128), jnp.float32),
            pltpu.VMEM((8, 128), jnp.float32),
            pltpu.VMEM((32, 8, 128), jnp.float32),
            pltpu.VMEM((8, 128), jnp.float32),
            pltpu.VMEM((8, 8, 128), jnp.float32),
            pltpu.SemaphoreType.DMA((64,)),
            pltpu.SemaphoreType.DMA,
            pltpu.SemaphoreType.DMA((NQ, 8, 2)),
            pltpu.SemaphoreType.DMA,
            pltpu.SemaphoreType.DMA,
            pltpu.SemaphoreType.DMA,
            pltpu.SemaphoreType.DMA,
            pltpu.SemaphoreType.DMA((3,)),
            pltpu.SemaphoreType.DMA((3,)),
        ],
        compiler_params=pltpu.CompilerParams(
            collective_id=0, has_side_effects=True, vmem_limit_bytes=60 * 2**20),
        name="gather_and_score",
    )(hidden, weight, labels, mask)


def shards(hidden, out_weight, labels, text_mask):
    loss, mean = scored(hidden, out_weight, labels.reshape(5, 128), text_mask.reshape(5, 128))
    return (loss.reshape(-1), mean[0, 0])


def solution(mesh):
    in_specs = (P(("dp", "vocab"), None), P("dp", "vocab"), P("dp"), P("dp"))
    out_specs = (P("dp"), P())
    return jax.shard_map(shards, mesh=mesh, in_specs=in_specs, out_specs=out_specs, check_vma=False)
```

time: 182 us -> 124 us (0.68)
  blocking collectives: 39 us -> 0 us
  Pallas kernels: 133 us -> 120 us
  other arithmetic: 3.76 us -> 0 us
  local copies, waits for them, and re-layouts: 3.18 us -> 1.26 us
    all_to_all x3 -> x0, blocking collectives: 39 us -> none  [the longest x2 27.7 us: from_everyone(): lax.all_to_all(jnp.broadcast_to(x[None], (devices, *x.shape)), axis, 0, 0...]
    pallas_call x1, Pallas kernels: 133 us -> 120 us  [scored(): pl.pallas_call(main_kernel, out_shape=(jax.ShapeDtypeStruct((5, 128), jnp...]
where the time goes in v2:
time: 124 us
  Pallas kernels  120 us (97%)
  between operations  2.4 us (2%)
  local copies, waits for them, and re-layouts  1.26 us (1%)
    pallas_call x1, Pallas kernels, scored(): pl.pallas_call(main_kernel, out_shape=(jax.ShapeDtypeStruct((5, 128), jnp...  120 us

profile of v2, /device:TPU:1, one launch (start us, length us, event | category | flops | bytes accessed | tf_op | source)
XLA Modules:
  0.0 123.8 jit_solution(9964792677719696469)
XLA Ops:
  0.6 120.2 %gather_and_score.1 = (f32[5,128]{1,0:T(8,128)}, f32[1,1]{1,0:T(1,128)}) custom-call(bf16[20,4096]{1,0:T(8,128)(2,1)} %h_ref.1, bf16[512,2560]{1,0:T(8,128)(2,1)} %w_ref.1, s32[5,128]{1,0:T(8,128)} %bitcast.4, s32[5,128]{1,0:T(8,128)} %bitcast.5), custom_call_target="tpu_custom_call" | custom-call | tf_op jit(solution)/shard_map/gather_and_score/pallas_call | solution.py:481
  120.8 1.3 %copy.8 = f32[640]{0:T(1024)} copy(f32[640]{0:T(1024)} %bitcast.6) | data formatting | bytes 5120

commit v3 on v2

--- a/solution.py
+++ b/solution.py
@@ -17,18 +17,18 @@
 TOK = 8 * GROUP
 LEAST = float(jnp.finfo(jnp.float32).min)
 MT = 320
-RING = (8, 8, 18, 18, 27, 27, 42)
+RING = (8, 8, 16, 16, 27, 27, 42)
 SPREAD = (8, 13, 20, 27, 34, 42, 50)
-ROUND1 = (6, 14, 20, 28, 35, 43, 51, 58)
+ROUND1 = (6, 16, 20, 28, 35, 43, 51, 58)
 ROUND2 = (18, 25, 32, 38, 46, 53, 60, 66)
-ROUND3 = (26, 34, 42, 49, 57, 63, 69, 75)
+ROUND3 = (26, 34, 42, 45, 53, 59, 66, 71)
 SEND = (0, 8, 18, 27, 32, 37, 43, 48, 53, 58)
 DIRECT = (12, 20, 29, 37, 43, 48, 54, 60, 65, 71)
 ACROSS = (21, 29, 38, 46, 52, 57, 63, 69, 74, 80)
-OTHER = (31, 48, 59, 71, 82)
-CELLS = ((0, 0, 40), (1, 0, 52), (0, 1, 52), (1, 1, 56), (0, 2, 60), (1, 2, 64), (2, 0, 64), (2, 1, 68), (2, 2, 68), (0, 3, 72), (1, 3, 72), (2, 3, 76), (3, 0, 76), (3, 1, 76), (3, 2, 77), (3, 3, 77))
+OTHER = (31, 52, 66, 74, 84)
+CELLS = ((0, 0, 36), (1, 0, 48), (0, 1, 52), (1, 1, 56), (2, 0, 60), (2, 1, 64), (0, 2, 66), (1, 2, 67), (2, 2, 67), (3, 0, 74), (0, 3, 75), (1, 3, 75), (3, 1, 76), (2, 3, 76), (3, 2, 80), (3, 3, 80))
 STEP_US = 4
-STEPS = 82 // STEP_US + 1
+STEPS = 84 // STEP_US + 1
 MESH = pl.DeviceIdType.MESH
 
 
@@ -286,7 +286,7 @@
     col_b = (ystar * 4 + x) * (8 * BLOCK) + z * BLOCK
 
     def cell(t, q):
-        rows = pl.ds(pl.multiple_of(t * MT, MT), MT)
+        rows = pl.ds(t * MT if isinstance(t, int) else pl.multiple_of(t * MT, MT), MT)
         logits = jnp.dot(act[rows, :], wbuf[q], preferred_element_type=jnp.float32)
         a, b = logits[:, :CH], logits[:, CH:]
         target = labcol[rows, :] - lane
@@ -383,10 +383,10 @@
 
     ids = lax.broadcasted_iota(jnp.int32, (128, 128), 1)
 
-    def to_owner(d):
+    def pack(d):
         columns = []
         for base, size in ((0, 128), (128, 32)):
-            rows = pl.ds(pl.multiple_of(d * GROUP + base, 32), size)
+            rows = pl.ds(d * GROUP + base, size)
             m = m_ref[rows, :]
             top = jnp.max(m, axis=1, keepdims=True)
             total = jnp.sum(s_ref[rows, :] * jnp.exp(m - top), axis=1, keepdims=True)
@@ -399,18 +399,20 @@
             packed = jnp.where(ids == 2 * k + 1, jnp.concatenate([columns[1][k], fill], axis=0), packed)
         out1[d] = jnp.transpose(packed)[:8]
 
-        @pl.when(d > 0)
-        def _():
-            pltpu.make_async_remote_copy(
-                src_ref=out1.at[d], dst_ref=in1.at[z], send_sem=fsend.at[0], recv_sem=frecv.at[0],
-                device_id=dev(z_of(d), y, x, c), device_id_type=MESH).start()
-
-    @pl.loop(0, 4)
-    def _(k):
-        t = 3 - k
-        cell(t, NQ - 1)
-        to_owner(2 * t + 1)
-        to_owner(2 * t)
+    def to_owner(d):
+        pltpu.make_async_remote_copy(
+            src_ref=out1.at[d], dst_ref=in1.at[z], send_sem=fsend.at[0], recv_sem=frecv.at[0],
+            device_id=dev(z_of(d), y, x, c), device_id_type=MESH).start()
+
+    for k in range(5):
+        if k < 4:
+            cell(3 - k, NQ - 1)
+        if k > 0:
+            for d in (9 - 2 * k, 8 - 2 * k):
+                pack(d)
+            for d in (9 - 2 * k, 8 - 2 * k):
+                if d > 0:
+                    to_owner(d)
 
     in1[z] = out1[0]
     seven = in1.at[pl.ds(0, 7)]
@@ -421,11 +423,11 @@
     out2[4:6, :] = got
     out2[6:8, :] = got
 
-    @pl.loop(1, 32)
+    @pl.loop(20, 51)
     def _(k):
         pltpu.make_async_remote_copy(
             src_ref=out2, dst_ref=in2.at[v], send_sem=fsend.at[1], recv_sem=frecv.at[1],
-            device_id={"dp": z, "vocab": (v + k) % 32}, device_id_type=MESH).start()
+            device_id={"dp": z, "vocab": (v + k + k // 32) % 32}, device_id_type=MESH).start()
 
     in2[v] = out2[...]
     many = in2.at[pl.ds(0, 31)]
@@ -435,14 +437,13 @@
             tiles = [in2[((pair * 2 + k // 4) * 4 + k % 4) * 2 + core] for k in range(8)]
             top, total, got = joined(tiles)
             at = (pair * 2 + core) * 2
-            loss_in[at : at + 2, :] = mask_in[at : at + 2, :] * (top + jnp.log(total) - got)
-    loss_sum = jnp.sum(loss_in[...], axis=(0, 1), keepdims=True)
+            loss_in[at : at + 2, :] = top + jnp.log(total) - got
+    loss_sum = jnp.sum(mask_in[...] * loss_in[...], axis=(0, 1), keepdims=True)
     tally = jnp.sum(mask_in[...], axis=(0, 1), keepdims=True)
     out3[0:4, :] = jnp.broadcast_to(loss_sum, (4, 128))
     out3[4:8, :] = jnp.broadcast_to(tally, (4, 128))
 
-    @pl.loop(1, 8)
-    def _(k):
+    for k in (4, 3, 5, 2, 6, 1, 7):
         pltpu.make_async_remote_copy(
             src_ref=out3, dst_ref=in3.at[z], send_sem=fsend.at[2], recv_sem=frecv.at[2],
             device_id=dev((z + k) % 8, y, x, c), device_id_type=MESH).start()
@@ -522,7 +523,7 @@
 
 def shards(hidden, out_weight, labels, text_mask):
     loss, mean = scored(hidden, out_weight, labels.reshape(5, 128), text_mask.reshape(5, 128))
-    return (loss.reshape(-1), mean[0, 0])
+    return (text_mask.astype(jnp.float32) * loss.reshape(-1), mean[0, 0])
 
 
 def solution(mesh):

time: 124 us -> 123 us (level)
  other arithmetic: 0 us -> 1.27 us
  local copies, waits for them, and re-layouts: 1.26 us -> 0.01 us
    mul x0 -> x1, other arithmetic: none -> 1.27 us  [shards(): return (text_mask.astype(jnp.float32) * loss.reshape(-1), mean[0, 0])]
    unnamed x1 -> x2, local copies, waits for them, and re-layouts: 1.26 us -> 0.01 us
where the time goes in v3:
time: 123 us
  Pallas kernels  119 us (97%)
  between operations  2.42 us (2%)
  other arithmetic  1.27 us (1%)
    pallas_call x1, Pallas kernels, scored(): pl.pallas_call(main_kernel, out_shape=(jax.ShapeDtypeStruct((5, 128), jnp...  119 us

profile of v3, /device:TPU:1, one launch (start us, length us, event | category | flops | bytes accessed | tf_op | source)
XLA Modules:
  0.0 122.9 jit_solution(568226892150117391)
XLA Ops:
  0.6 0.0 copy-start
  0.6 119.2 %gather_and_score.1 = (f32[5,128]{1,0:T(8,128)}, f32[1,1]{1,0:T(1,128)}) custom-call(bf16[20,4096]{1,0:T(8,128)(2,1)} %h_ref.1, bf16[512,2560]{1,0:T(8,128)(2,1)} %w_ref.1, s32[5,128]{1,0:T(8,128)} %bitcast.6, s32[5,128]{1,0:T(8,128)} %bitcast.5), custom_call_target="tpu_custom_call" | custom-call | tf_op jit(solution)/shard_map/gather_and_score/pallas_call | solution.py:482
  119.9 0.0 copy-done
  119.9 1.3 %bitcast_multiply_fusion = f32[640]{0:T(1024)} fusion(f32[5,128]{1,0:T(8,128)} %get-tuple-element.4, s32[640]{0:T(1024)S(1)} %copy-done), kind=kLoop, calls=%fused_computation | loop fusion | flops 1280 | bytes 7680 | tf_op jit(solution)/shard_map/mul | solution.py:526
Async XLA Ops:
  0.6 119.3 %copy-start = (s32[640]{0:T(1024)S(1)}, s32[640]{0:T(1024)}, u32[]{:S(2)}) copy-start(s32[640]{0:T(1024)} %param.7) | copy-start | bytes 7684

commit v4 on v3

--- a/solution.py
+++ b/solution.py
@@ -95,6 +95,45 @@
         stage[kq * 4 : kq * 4 + 4, 0 : D // 4] = few[:, kq * (D // 4) : (kq + 1) * (D // 4)]
     braw[own] = stage[:, 0 : D // 4].astype(jnp.bfloat16)
     first.wait()
+
+    def place(t):
+        piece = (t * 3277) >> 16
+        r = t - piece * ROWS
+        s8 = ((piece >> 1) & 3) * 2 + ((piece >> 3) & 1)
+        group = (piece >> 4) * 2 + (piece & 1)
+        head = r < 16
+        return jnp.where(head, s8 * 16 + r, s8 * 4 + r - 16), group * 2 + jnp.where(head, 0, 1)
+
+    tile_row = lax.broadcasted_iota(jnp.int32, (8, 128), 0)
+    tile_lane = lax.broadcasted_iota(jnp.int32, (8, 128), 1)
+
+    def is_row(k):
+        return place(k * 128 + tile_lane)[1] == tile_row
+
+    for k in range(5):
+        ids = lax.broadcasted_iota(jnp.int32, (128, 128), 0) + k * 128
+        lanes = lax.broadcasted_iota(jnp.int32, (128, 128), 1)
+        perm[k] = jnp.where(place(ids)[0] == lanes, 1.0, 0.0)
+
+    def by_piece(ref):
+        out = jnp.zeros((8, 128), jnp.float32)
+        for k in range(5):
+            line = jnp.broadcast_to(ref[k : k + 1].astype(jnp.float32), (8, 128))
+            out += jnp.dot(
+                jnp.where(is_row(k), line, 0.0), perm[k],
+                preferred_element_type=jnp.float32, precision=lax.Precision.HIGHEST)
+        return out
+
+    mask_in[...] = by_piece(mask_ref)
+    labels = by_piece(lab_ref)
+    group = (y // 2) * 2 + c
+    lines = [
+        jnp.sum(jnp.where(tile_row == group * 2 + k, labels, 0.0), axis=0, keepdims=True) for k in range(2)
+    ]
+    lab_out[...] = jnp.where(tile_row == 0, lines[0], lines[1]).astype(jnp.int32)
+    m_ref[...] = jnp.full_like(m_ref, LEAST)
+    s_ref[...] = jnp.zeros_like(s_ref)
+    p_ref[...] = jnp.zeros_like(p_ref)
     pl.semaphore_wait(bar, 45)
 
     def h_copy(d, piece, to_d, device):
@@ -301,42 +340,6 @@
     ring(jnp.int32(0))
     step_a(jnp.int32(0))
 
-    def place(t):
-        piece = (t * 3277) >> 16
-        r = t - piece * ROWS
-        s8 = ((piece >> 1) & 3) * 2 + ((piece >> 3) & 1)
-        group = (piece >> 4) * 2 + (piece & 1)
-        head = r < 16
-        return jnp.where(head, s8 * 16 + r, s8 * 4 + r - 16), group * 2 + jnp.where(head, 0, 1)
-
-    tile_row = lax.broadcasted_iota(jnp.int32, (8, 128), 0)
-    tile_lane = lax.broadcasted_iota(jnp.int32, (8, 128), 1)
-
-    def is_row(k):
-        return place(k * 128 + tile_lane)[1] == tile_row
-
-    for k in range(5):
-        ids = lax.broadcasted_iota(jnp.int32, (128, 128), 0) + k * 128
-        lanes = lax.broadcasted_iota(jnp.int32, (128, 128), 1)
-        perm[k] = jnp.where(place(ids)[0] == lanes, 1.0, 0.0)
-
-    def by_piece(ref):
-        out = jnp.zeros((8, 128), jnp.float32)
-        for k in range(5):
-            line = jnp.broadcast_to(ref[k : k + 1].astype(jnp.float32), (8, 128))
-            out += jnp.dot(
-                jnp.where(is_row(k), line, 0.0), perm[k],
-                preferred_element_type=jnp.float32, precision=lax.Precision.HIGHEST)
-        return out
-
-    mask_in[...] = by_piece(mask_ref)
-    labels = by_piece(lab_ref)
-    group = (y // 2) * 2 + c
-    lines = [
-        jnp.sum(jnp.where(tile_row == group * 2 + k, labels, 0.0), axis=0, keepdims=True) for k in range(2)
-    ]
-    lab_out[...] = jnp.where(tile_row == 0, lines[0], lines[1]).astype(jnp.int32)
-
     @pl.loop(1, 8)
     def _(k):
         pltpu.make_async_remote_copy(
@@ -344,9 +347,6 @@
             device_id=dev((z + k) % 8, y, x, c), device_id_type=MESH).start()
 
     labs[z] = lab_out[...]
-    m_ref[...] = jnp.full_like(m_ref, LEAST)
-    s_ref[...] = jnp.zeros_like(s_ref)
-    p_ref[...] = jnp.zeros_like(p_ref)
 
     def at_step(i, times, body):
         ready = [sum(1 for k in times if k // STEP_US < n) for n in range(STEPS + 1)]

time: 123 us -> 123 us (level)
  no operation moved by 1% of the time
where the time goes in v4:
time: 123 us
  Pallas kernels  119 us (97%)
  between operations  2.42 us (2%)
  other arithmetic  1.27 us (1%)
    pallas_call x1, Pallas kernels, scored(): pl.pallas_call(main_kernel, out_shape=(jax.ShapeDtypeStruct((5, 128), jnp...  119 us

profile of v4, /device:TPU:1, one launch (start us, length us, event | category | flops | bytes accessed | tf_op | source)
XLA Modules:
  0.0 122.9 jit_solution(17036986203279572069)
XLA Ops:
  0.6 0.0 copy-start
  0.6 119.2 %gather_and_score.1 = (f32[5,128]{1,0:T(8,128)}, f32[1,1]{1,0:T(1,128)}) custom-call(bf16[20,4096]{1,0:T(8,128)(2,1)} %h_ref.1, bf16[512,2560]{1,0:T(8,128)(2,1)} %w_ref.1, s32[5,128]{1,0:T(8,128)} %bitcast.6, s32[5,128]{1,0:T(8,128)} %bitcast.5), custom_call_target="tpu_custom_call" | custom-call | tf_op jit(solution)/shard_map/gather_and_score/pallas_call | solution.py:482
  119.8 0.0 copy-done
  119.9 1.3 %bitcast_multiply_fusion = f32[640]{0:T(1024)} fusion(f32[5,128]{1,0:T(8,128)} %get-tuple-element.4, s32[640]{0:T(1024)S(1)} %copy-done), kind=kLoop, calls=%fused_computation | loop fusion | flops 1280 | bytes 7680 | tf_op jit(solution)/shard_map/mul | solution.py:526
Async XLA Ops:
  0.6 119.2 %copy-start = (s32[640]{0:T(1024)S(1)}, s32[640]{0:T(1024)}, u32[]{:S(2)}) copy-start(s32[640]{0:T(1024)} %param.7) | copy-start | bytes 7684
